TPU v7x, 512 devices: a whole 4x4x16 slice. The times are simulated.
512 devices in a mesh: section: 16 (over z), expert: 32 (over x, y, core).
Axes of the slice: x: 4, y: 4, z: 16, core: 2. Of those that a mesh axis runs over, the one named last changes fastest.
Arguments:
- section_in: bfloat16 [16, 1024, 2048], P('section', 'expert'), may hold values from -6 to 6
- new_batch: bfloat16 [1, 1024, 2048], P(None, 'expert'), may hold values from -6 to 6
- stashed: bfloat16 [2, 16, 1024, 2048], P(None, 'section', 'expert'), may hold values from -6 to 6
- grad_in: bfloat16 [16, 1024, 2048], P('section', 'expert'), may hold values from -6 to 6
- loss_grad: bfloat16 [1, 1024, 2048], P(None, 'expert'), may hold values from -6 to 6
- routes: int32 [2, 2, 16, 1024, 2], P(None, None, 'section', 'expert'), may hold values from 0 to 7, all different within a row; in each aligned block of 32 rows (0 to 31, 32 to 63, ..., all dimensions but the last counted through in order) at most 8 rows name the same one
- counts: int32 [2, 2, 16, 1024], P(None, None, 'section', 'expert'), may hold values from 0 to 2, as said below
- norm_gain: float32 [16, 2048], P('section'), may hold values from 0.1 to 1.9
- w_router: bfloat16 [16, 2048, 8], P('section'), may hold values from -0.125 to 0.125
- w_gate: bfloat16 [16, 2048, 8192], P('section', None, 'expert'), may hold values from -0.125 to 0.125
- w_up: bfloat16 [16, 2048, 8192], P('section', None, 'expert'), may hold values from -0.125 to 0.125
- w_down: bfloat16 [16, 8192, 2048], P('section', 'expert'), may hold values from -0.1875 to 0.1875
- lam: float32 [16], P('section'), may hold values from 4 to 40
Outputs:
- fwd_out: bfloat16 [2, 16, 1024, 2048], P(None, 'section', 'expert')
- grad_out: bfloat16 [2, 16, 1024, 2048], P(None, 'section', 'expert')
- lam_out: float32 [16], P('section')
Inputs may be any that keep to these rules, and one draw needn't show every extreme that they name: routes[m, k, s, t] names 2 different experts; among the 32 tokens of one device's aligned block no expert is named more than 8 times. counts[m, k, s, t] active entries come first in the token's list.
All inputs are finite; a program needn't handle non-finite values.
Results may differ from a plain program's by a relative error of at most 0.01.
Values may be sent and summed in bfloat16 or wider, within the bound.
A program may use at most 128 MiB of HBM per device.

v0:
```python
import jax
import jax.numpy as jnp
from jax import lax
from jax.sharding import PartitionSpec as P

SPLIT = 4
TICKS = 2


def shortened(value):

    def short(part):
        return part.astype(jnp.bfloat16) if part.dtype == jnp.float32 else part

    return jax.tree.map(short, value)


def from_behind(block, axis, distance):
    devices = range(lax.axis_size(axis))
    route = [(i - distance, i) for i in devices if i - distance in devices]
    return lax.ppermute(block, axis, route)


def norm_rows(values, gain_row):
    return values * lax.rsqrt(jnp.mean(values * values, axis=-1, keepdims=True) + 1e-05) * gain_row


def quarter_work(rows_f, rows_b, grads, scales, gate_q, up_q, down_q):
    all_rows = jnp.concatenate([rows_f, rows_b], axis=0)
    pre_gate = jnp.dot(all_rows, gate_q, preferred_element_type=jnp.float32)
    pre_up = jnp.dot(all_rows, up_q, preferred_element_type=jnp.float32)
    activated = jax.nn.silu(pre_gate)
    hidden = (activated * pre_up).astype(jnp.bfloat16)
    projected = jnp.dot(hidden, down_q, preferred_element_type=jnp.float32).astype(jnp.bfloat16)
    half_rows = rows_f.shape[0]
    scaled = (scales.astype(jnp.float32)[:, None] * grads.astype(jnp.float32)).astype(jnp.bfloat16)
    back_h = jnp.dot(scaled, down_q.T, preferred_element_type=jnp.float32)
    gate_tail = pre_gate[half_rows:]
    sigmoid_g = jax.nn.sigmoid(gate_tail)
    silu_slope = sigmoid_g * (1.0 + gate_tail * (1.0 - sigmoid_g))
    d_gate = (back_h * pre_up[half_rows:] * silu_slope).astype(jnp.bfloat16)
    d_up = (back_h * activated[half_rows:]).astype(jnp.bfloat16)
    d_rows = (
        jnp.dot(d_gate, gate_q.T, preferred_element_type=jnp.float32)
        + jnp.dot(d_up, up_q.T, preferred_element_type=jnp.float32)
    ).astype(jnp.bfloat16)
    inner_dot = jnp.sum(
        grads.astype(jnp.float32) * projected[half_rows:].astype(jnp.float32), axis=-1
    ).astype(jnp.bfloat16)
    return (projected[:half_rows], d_rows, inner_dot)


def slot_tables(route, count, experts, capacity):
    tok_rows, top_slots = route.shape
    flat_list = route.reshape(tok_rows * top_slots)
    onehot = (flat_list[:, None] == jnp.arange(experts, dtype=jnp.int32)[None, :]).astype(jnp.int32)
    slot_rank = jnp.sum((jnp.cumsum(onehot, axis=0) - 1) * onehot, axis=1)
    target = (flat_list * capacity + slot_rank).reshape(tok_rows, top_slots)
    live_mask = jnp.arange(top_slots, dtype=jnp.int32)[None, :] < count[:, None]
    slot_table = (
        (target[:, :, None] == jnp.arange(experts * capacity, dtype=jnp.int32)[None, None, :])
        & live_mask[:, :, None]
    ).astype(jnp.bfloat16)
    return (slot_table, target, live_mask.astype(jnp.float32))


def route_rows(rows_f, rows_b, grads_b, scales_b, experts, capacity, gate_cols, up_cols, down_rows):
    width = rows_f.shape[-1]

    def work(got_f, got_b, got_g, got_s):
        leading = got_f.shape[:-1]
        projected, d_rows, inner_dot = quarter_work(
            got_f.reshape(-1, width),
            got_b.reshape(-1, width),
            got_g.reshape(-1, width),
            got_s.reshape(-1),
            gate_cols,
            up_cols,
            down_rows,
        )
        return (
            projected.reshape(leading + (width,)),
            d_rows.reshape(leading + (width,)),
            inner_dot.reshape(leading),
        )

    grouped_rows = (
        rows_f.reshape((experts, capacity, width)),
        rows_b.reshape((experts, capacity, width)),
        grads_b.reshape((experts, capacity, width)),
        scales_b.reshape((experts, capacity)),
    )
    outgoing = tuple(
        (
            jnp.broadcast_to(
                element.reshape((experts, 1) + element.shape[1:]),
                (experts, SPLIT) + element.shape[1:],
            ).reshape((experts * SPLIT,) + element.shape[1:])
            for element in grouped_rows
        )
    )
    received = jax.tree.map(
        lambda part, own: part.astype(own.dtype),
        lax.all_to_all(shortened(outgoing), "expert", split_axis=0, concat_axis=0, tiled=True),
        outgoing,
    )
    returned = lax.all_to_all(
        shortened(work(*received)), "expert", split_axis=0, concat_axis=0, tiled=True
    )
    return tuple(
        (
            jnp.sum(
                element.astype(jnp.float32).reshape((experts, SPLIT, capacity) + element.shape[2:]),
                axis=1,
            ).reshape((experts * capacity,) + element.shape[2:])
            for element in returned
        )
    )


def on_device(
    section_in,
    new_batch,
    stashed,
    grad_in,
    loss_grad,
    routes,
    counts,
    norm_gain,
    w_router,
    w_gate,
    w_up,
    w_down,
    lam,
):
    section_pos = lax.axis_index("section")
    last_section = lax.axis_size("section") - 1
    tok_rows = section_in.shape[1]
    top_slots = routes.shape[-1]
    experts = w_router.shape[-1]
    capacity = SPLIT * min(
        tok_rows // (2 * SPLIT), 5 * tok_rows * top_slots // (4 * experts * SPLIT)
    )
    share_total = tok_rows * lax.axis_size("expert") * top_slots
    gain_row = norm_gain[0]
    router = w_router[0]
    gate_cols = w_gate[0]
    up_cols = w_up[0]
    down_rows = w_down[0]
    totals = lax.psum(jnp.sum(counts[0, :, 0], axis=-1).astype(jnp.float32), "expert")
    weight = lam[0]
    forward_x = section_in[0]
    cotangent = grad_in[0]
    fwd_list = []
    grad_list = []
    for tick_num in range(TICKS):
        if tick_num > 0:
            arriving = from_behind(fwd_list[-1], "section", 1)
            forward_x = jnp.where(section_pos == 0, new_batch[tick_num - 1], arriving)
            coming = from_behind(grad_list[-1], "section", -1)
            cotangent = jnp.where(section_pos == last_section, loss_grad[tick_num - 1], coming)
        route_f = routes[0, tick_num, 0]
        route_b = routes[1, tick_num, 0]
        table_f, target_f, live_f = slot_tables(route_f, counts[0, tick_num, 0], experts, capacity)
        table_b, target_b, live_b = slot_tables(route_b, counts[1, tick_num, 0], experts, capacity)
        normed_f = norm_rows(forward_x.astype(jnp.float32), gain_row).astype(jnp.bfloat16)
        picked_f = jnp.take_along_axis(
            jnp.dot(normed_f, router, preferred_element_type=jnp.float32), route_f, axis=1
        )
        gate_f = jax.nn.softplus(picked_f) * live_f
        normed_raw, pullback = jax.vjp(
            lambda values: norm_rows(values, gain_row), stashed[tick_num, 0].astype(jnp.float32)
        )
        normed_b = normed_raw.astype(jnp.bfloat16)
        picked_b = jnp.take_along_axis(
            jnp.dot(normed_b, router, preferred_element_type=jnp.float32), route_b, axis=1
        )
        gate_b = jax.nn.softplus(picked_b) * live_b
        rows_f = jnp.einsum(
            "tjc,td->cd", table_f, normed_f, preferred_element_type=jnp.float32
        ).astype(jnp.bfloat16)
        rows_b = jnp.einsum(
            "tjc,td->cd", table_b, normed_b, preferred_element_type=jnp.float32
        ).astype(jnp.bfloat16)
        grads_b = jnp.einsum(
            "tjc,td->cd", table_b, cotangent, preferred_element_type=jnp.float32
        ).astype(jnp.bfloat16)
        scales_b = (
            jnp.zeros((experts * capacity,), jnp.float32)
            .at[target_b.reshape(-1)]
            .add(gate_b.reshape(-1))
            .astype(jnp.bfloat16)
        )
        y_slots, dn_slots, dot_slots = route_rows(
            rows_f, rows_b, grads_b, scales_b, experts, capacity, gate_cols, up_cols, down_rows
        )
        y_tok = jnp.take(y_slots, target_f, axis=0)
        out_f = (
            forward_x.astype(jnp.float32) + jnp.sum(gate_f[:, :, None] * y_tok, axis=1)
        ).astype(jnp.bfloat16)
        dpick = (jnp.take(dot_slots, target_b, axis=0) + weight) * jax.nn.sigmoid(picked_b) * live_b
        onehot_b = (
            route_b[:, :, None] == jnp.arange(experts, dtype=jnp.int32)[None, None, :]
        ).astype(jnp.float32)
        dlogit = jnp.sum(onehot_b * dpick[:, :, None], axis=1)
        dnorm = jnp.sum(
            live_b[:, :, None] * jnp.take(dn_slots, target_b, axis=0), axis=1
        ) + jnp.dot(dlogit, router.astype(jnp.float32).T, precision=lax.Precision.HIGHEST)
        grad_x = (cotangent.astype(jnp.float32) + pullback(dnorm)[0]).astype(jnp.bfloat16)
        fwd_list.append(out_f)
        grad_list.append(grad_x)
        weight = weight * jnp.exp(4.0 * (totals[tick_num] / share_total - 0.5))
    return (jnp.stack(fwd_list)[:, None], jnp.stack(grad_list)[:, None], weight.reshape(1))


def solution(mesh):
    in_specs = (
        P("section", "expert", None),
        P(None, "expert", None),
        P(None, "section", "expert", None),
        P("section", "expert", None),
        P(None, "expert", None),
        P(None, None, "section", "expert", None),
        P(None, None, "section", "expert"),
        P("section", None),
        P("section", None, None),
        P("section", None, "expert"),
        P("section", None, "expert"),
        P("section", "expert", None),
        P("section"),
    )
    out_specs = (
        P(None, "section", "expert", None),
        P(None, "section", "expert", None),
        P("section"),
    )
    return jax.shard_map(
        on_device, mesh=mesh, in_specs=in_specs, out_specs=out_specs, check_vma=False
    )
```

profile of v0, /device:TPU:1, one launch (start us, length us, event | category | flops | bytes accessed | tf_op | source)
XLA Modules:
  0.0 372.0 jit_solution(5309016546662161397)
XLA Ops:
  0.6 1.1 fusion.59
  1.8 1.3 slice_bitcast_fusion.3
  3.1 1.3 slice_bitcast_fusion.6
  6.5 1.3 compare_select_fusion.2
  8.4 1.2 fusion.5
  10.8 10.5 %all-to-all-start.1 = ((bf16[32,8,2048]{2,1,0:T(8,128)(2,1)}), bf16[32,8,2048]{2,1,0:T(8,128)(2,1)S(1)}, u32[]{:S(2)}, u32[]{:S(2)}) async-start(bf16[32,8,2048]{2,1,0:T(8,128)(2,1)} %bitcast.14), calls=%async_computation.1 | async-start | bytes 2097152 | tf_op jit(solution)/shard_map/all_to_all | solution.py:104
  25.6 12.6 %all-to-all-done.1 = bf16[32,8,2048]{2,1,0:T(8,128)(2,1)S(1)} async-done(((bf16[32,8,2048]{2,1,0:T(8,128)(2,1)}), bf16[32,8,2048]{2,1,0:T(8,128)(2,1)S(1)}, u32[]{:S(2)}, u32[]{:S(2)}) %all-to-all-start.1) | async-done | bytes 1048608 | tf_op jit(solution)/shard_map/all_to_all | solution.py:104
  38.2 1.2 broadcast_in_dim.59
  39.5 4.4 %all-to-all-start = ((bf16[32,8,2048]{2,1,0:T(8,128)(2,1)}), bf16[32,8,2048]{2,1,0:T(8,128)(2,1)}, u32[]{:S(2)}, u32[]{:S(2)}) async-start(bf16[32,8,2048]{2,1,0:T(8,128)(2,1)} %bitcast.8), calls=%async_computation | async-start | bytes 2097152 | tf_op jit(solution)/shard_map/all_to_all | solution.py:104
  44.0 1.5 slice_reduce_fusion
  48.6 12.3 %all-to-all-done = bf16[32,8,2048]{2,1,0:T(8,128)(2,1)} async-done(((bf16[32,8,2048]{2,1,0:T(8,128)(2,1)}), bf16[32,8,2048]{2,1,0:T(8,128)(2,1)}, u32[]{:S(2)}, u32[]{:S(2)}) %all-to-all-start) | async-done | bytes 1048608 | tf_op jit(solution)/shard_map/all_to_all | solution.py:104
  62.1 3.9 %all-to-all-start.7 = ((bf16[32,8,2048]{2,1,0:T(8,128)(2,1)}), bf16[32,8,2048]{2,1,0:T(8,128)(2,1)S(1)}, u32[]{:S(2)}, u32[]{:S(2)}) async-start(bf16[32,8,2048]{2,1,0:T(8,128)(2,1)} %bitcast.50), calls=%async_computation.7 | async-start | bytes 2097152 | tf_op jit(solution)/shard_map/all_to_all | solution.py:104
  67.4 1.2 convert_element_type.390
  68.5 1.4 copy.243
  69.9 2.4 fusion.20
  72.3 2.9 divide_multiply_fusion.1
  75.3 2.1 convolution_convert_fusion.1
  77.4 5.6 %all-to-all-done.7 = bf16[32,8,2048]{2,1,0:T(8,128)(2,1)S(1)} async-done(((bf16[32,8,2048]{2,1,0:T(8,128)(2,1)}), bf16[32,8,2048]{2,1,0:T(8,128)(2,1)S(1)}, u32[]{:S(2)}, u32[]{:S(2)}) %all-to-all-start.7) | async-done | bytes 1048608 | tf_op jit(solution)/shard_map/all_to_all | solution.py:104
  83.0 1.6 fusion.14
  85.2 4.0 %all-to-all-start.9 = ((bf16[32,1,8]{2,1,0:T(2,128)(2,1)}), bf16[32,1,8]{2,1,0:T(2,128)(2,1)S(1)}, u32[]{:S(2)}, u32[]{:S(2)}) async-start(bf16[32,1,8]{2,1,0:T(2,128)(2,1)} %convert_element_type.401), calls=%async_computation.9 | async-start | bytes 32768 | tf_op jit(solution)/shard_map/all_to_all | solution.py:107
  91.4 4.7 %all-to-all-done.9 = bf16[32,1,8]{2,1,0:T(2,128)(2,1)S(1)} async-done(((bf16[32,1,8]{2,1,0:T(2,128)(2,1)}), bf16[32,1,8]{2,1,0:T(2,128)(2,1)S(1)}, u32[]{:S(2)}, u32[]{:S(2)}) %all-to-all-start.9) | async-done | bytes 544 | tf_op jit(solution)/shard_map/all_to_all | solution.py:107
  99.8 4.1 %all-to-all-start.6 = ((bf16[32,1,8]{2,1,0:T(2,128)(2,1)}), bf16[32,1,8]{2,1,0:T(2,128)(2,1)S(1)}, u32[]{:S(2)}, u32[]{:S(2)}) async-start(bf16[32,1,8]{2,1,0:T(2,128)(2,1)} %copy.246), calls=%async_computation.6 | async-start | bytes 32768 | tf_op jit(solution)/shard_map/all_to_all | solution.py:104
  104.0 2.3 slice_bitcast_fusion.1
  106.3 4.6 %all-to-all-done.6 = bf16[32,1,8]{2,1,0:T(2,128)(2,1)S(1)} async-done(((bf16[32,1,8]{2,1,0:T(2,128)(2,1)}), bf16[32,1,8]{2,1,0:T(2,128)(2,1)S(1)}, u32[]{:S(2)}, u32[]{:S(2)}) %all-to-all-start.6) | async-done | bytes 544 | tf_op jit(solution)/shard_map/all_to_all | solution.py:104
  111.6 4.2 %all-to-all-start.2 = ((bf16[32,8,2048]{2,1,0:T(8,128)(2,1)}), bf16[32,8,2048]{2,1,0:T(8,128)(2,1)S(1)}, u32[]{:S(2)}, u32[]{:S(2)}) async-start(bf16[32,8,2048]{2,1,0:T(8,128)(2,1)} %slice_bitcast_fusion.1), calls=%async_computation.2 | async-start | bytes 2097152 | tf_op jit(solution)/shard_map/all_to_all | solution.py:107
  116.4 71.3 %psum.7 = f32[2]{0:T(128)} all-reduce(f32[2]{0:T(128)} %convert_element_type.390), channel_id=1, replica_groups=mesh['section'=16,'expert'=32] {'expert'}, use_global_device_ids=true, to_apply=%region_33.37 | all-reduce | flops 2 | bytes 16 | tf_op jit(solution)/shard_map/psum | solution.py:150
  187.7 1.3 copy.240
  189.7 1.4 mul.452
  191.9 1.3 copy.230
  194.1 1.5 convert_reduce_fusion.4
  198.2 1.5 fusion.3
  199.7 4.6 %all-to-all-start.8 = ((bf16[32,8,2048]{2,1,0:T(8,128)(2,1)}), bf16[32,8,2048]{2,1,0:T(8,128)(2,1)}, u32[]{:S(2)}, u32[]{:S(2)}) async-start(bf16[32,8,2048]{2,1,0:T(8,128)(2,1)} %fusion.3), calls=%async_computation.8 | async-start | bytes 2097152 | tf_op jit(solution)/shard_map/all_to_all | solution.py:107
  208.1 1.7 fusion.47
  209.8 11.4 %all-to-all-done.8 = bf16[32,8,2048]{2,1,0:T(8,128)(2,1)} async-done(((bf16[32,8,2048]{2,1,0:T(8,128)(2,1)}), bf16[32,8,2048]{2,1,0:T(8,128)(2,1)}, u32[]{:S(2)}, u32[]{:S(2)}) %all-to-all-start.8) | async-done | bytes 1048608 | tf_op jit(solution)/shard_map/all_to_all | solution.py:107
  221.2 1.4 convert_reduce_fusion.1
  223.8 1.7 fusion.45
  228.0 3.9 %all-to-all-start.4 = ((bf16[32,8,2048]{2,1,0:T(8,128)(2,1)}), bf16[32,8,2048]{2,1,0:T(8,128)(2,1)S(1)}, u32[]{:S(2)}, u32[]{:S(2)}) async-start(bf16[32,8,2048]{2,1,0:T(8,128)(2,1)} %bitcast.34), calls=%async_computation.4 | async-start | bytes 2097152 | tf_op jit(solution)/shard_map/all_to_all | solution.py:104
  232.7 1.6 collective-permute-start
  235.3 1.9 collective-permute-done
  238.4 10.5 %all-to-all-done.4 = bf16[32,8,2048]{2,1,0:T(8,128)(2,1)S(1)} async-done(((bf16[32,8,2048]{2,1,0:T(8,128)(2,1)}), bf16[32,8,2048]{2,1,0:T(8,128)(2,1)S(1)}, u32[]{:S(2)}, u32[]{:S(2)}) %all-to-all-start.4) | async-done | bytes 1048608 | tf_op jit(solution)/shard_map/all_to_all | solution.py:104
  248.9 1.2 broadcast_in_dim.63
  250.1 4.4 %all-to-all-start.3 = ((bf16[32,8,2048]{2,1,0:T(8,128)(2,1)}), bf16[32,8,2048]{2,1,0:T(8,128)(2,1)}, u32[]{:S(2)}, u32[]{:S(2)}) async-start(bf16[32,8,2048]{2,1,0:T(8,128)(2,1)} %bitcast.28), calls=%async_computation.3 | async-start | bytes 2097152 | tf_op jit(solution)/shard_map/all_to_all | solution.py:104
  254.7 1.3 collective-permute-start.1
  261.7 9.8 %all-to-all-done.3 = bf16[32,8,2048]{2,1,0:T(8,128)(2,1)} async-done(((bf16[32,8,2048]{2,1,0:T(8,128)(2,1)}), bf16[32,8,2048]{2,1,0:T(8,128)(2,1)}, u32[]{:S(2)}, u32[]{:S(2)}) %all-to-all-start.3) | async-done | bytes 1048608 | tf_op jit(solution)/shard_map/all_to_all | solution.py:104
  272.6 3.9 %all-to-all-start.11 = ((bf16[32,8,2048]{2,1,0:T(8,128)(2,1)}), bf16[32,8,2048]{2,1,0:T(8,128)(2,1)S(1)}, u32[]{:S(2)}, u32[]{:S(2)}) async-start(bf16[32,8,2048]{2,1,0:T(8,128)(2,1)} %bitcast.67), calls=%async_computation.11 | async-start | bytes 2097152 | tf_op jit(solution)/shard_map/all_to_all | solution.py:104
  279.1 2.4 fusion.18
  281.5 2.9 divide_multiply_fusion
  285.3 2.1 convolution_convert_fusion
  287.4 6.1 %all-to-all-done.11 = bf16[32,8,2048]{2,1,0:T(8,128)(2,1)S(1)} async-done(((bf16[32,8,2048]{2,1,0:T(8,128)(2,1)}), bf16[32,8,2048]{2,1,0:T(8,128)(2,1)S(1)}, u32[]{:S(2)}, u32[]{:S(2)}) %all-to-all-start.11) | async-done | bytes 1048608 | tf_op jit(solution)/shard_map/all_to_all | solution.py:104
  293.5 1.6 fusion.17
  295.8 4.0 %all-to-all-start.13 = ((bf16[32,1,8]{2,1,0:T(2,128)(2,1)}), bf16[32,1,8]{2,1,0:T(2,128)(2,1)S(1)}, u32[]{:S(2)}, u32[]{:S(2)}) async-start(bf16[32,1,8]{2,1,0:T(2,128)(2,1)} %convert_element_type.402), calls=%async_computation.13 | async-start | bytes 32768 | tf_op jit(solution)/shard_map/all_to_all | solution.py:107
  300.9 5.8 %all-to-all-done.13 = bf16[32,1,8]{2,1,0:T(2,128)(2,1)S(1)} async-done(((bf16[32,1,8]{2,1,0:T(2,128)(2,1)}), bf16[32,1,8]{2,1,0:T(2,128)(2,1)S(1)}, u32[]{:S(2)}, u32[]{:S(2)}) %all-to-all-start.13) | async-done | bytes 544 | tf_op jit(solution)/shard_map/all_to_all | solution.py:107
  310.5 4.4 %all-to-all-start.10 = ((bf16[32,1,8]{2,1,0:T(2,128)(2,1)}), bf16[32,1,8]{2,1,0:T(2,128)(2,1)S(1)}, u32[]{:S(2)}, u32[]{:S(2)}) async-start(bf16[32,1,8]{2,1,0:T(2,128)(2,1)} %copy.257), calls=%async_computation.10 | async-start | bytes 32768 | tf_op jit(solution)/shard_map/all_to_all | solution.py:104
  314.9 2.3 slice_bitcast_fusion
  317.2 4.7 %all-to-all-done.10 = bf16[32,1,8]{2,1,0:T(2,128)(2,1)S(1)} async-done(((bf16[32,1,8]{2,1,0:T(2,128)(2,1)}), bf16[32,1,8]{2,1,0:T(2,128)(2,1)S(1)}, u32[]{:S(2)}, u32[]{:S(2)}) %all-to-all-start.10) | async-done | bytes 544 | tf_op jit(solution)/shard_map/all_to_all | solution.py:104
  322.5 4.2 %all-to-all-start.5 = ((bf16[32,8,2048]{2,1,0:T(8,128)(2,1)}), bf16[32,8,2048]{2,1,0:T(8,128)(2,1)S(1)}, u32[]{:S(2)}, u32[]{:S(2)}) async-start(bf16[32,8,2048]{2,1,0:T(8,128)(2,1)} %slice_bitcast_fusion), calls=%async_computation.5 | async-start | bytes 2097152 | tf_op jit(solution)/shard_map/all_to_all | solution.py:107
  326.8 1.6 fusion.77
  333.4 1.5 fusion.2
  334.8 8.9 %all-to-all-done.5 = bf16[32,8,2048]{2,1,0:T(8,128)(2,1)S(1)} async-done(((bf16[32,8,2048]{2,1,0:T(8,128)(2,1)}), bf16[32,8,2048]{2,1,0:T(8,128)(2,1)S(1)}, u32[]{:S(2)}, u32[]{:S(2)}) %all-to-all-start.5) | async-done | bytes 1048608 | tf_op jit(solution)/shard_map/all_to_all | solution.py:107
  343.8 4.4 %all-to-all-start.12 = ((bf16[32,8,2048]{2,1,0:T(8,128)(2,1)}), bf16[32,8,2048]{2,1,0:T(8,128)(2,1)}, u32[]{:S(2)}, u32[]{:S(2)}) async-start(bf16[32,8,2048]{2,1,0:T(8,128)(2,1)} %fusion.2), calls=%async_computation.12 | async-start | bytes 2097152 | tf_op jit(solution)/shard_map/all_to_all | solution.py:107
  349.5 1.7 fusion.46
  352.0 13.2 %all-to-all-done.12 = bf16[32,8,2048]{2,1,0:T(8,128)(2,1)} async-done(((bf16[32,8,2048]{2,1,0:T(8,128)(2,1)}), bf16[32,8,2048]{2,1,0:T(8,128)(2,1)}, u32[]{:S(2)}, u32[]{:S(2)}) %all-to-all-start.12) | async-done | bytes 1048608 | tf_op jit(solution)/shard_map/all_to_all | solution.py:107
  365.2 1.4 convert_reduce_fusion
  367.8 1.7 fusion.44
  (365 shorter events, 59.7 us)
Async XLA Ops:
  0.6 74.7 %copy-start = (bf16[1,256,2048]{2,1,0:T(8,128)(2,1)S(1)}, bf16[1,256,2048]{2,1,0:T(8,128)(2,1)}, u32[]{:S(2)}) copy-start(bf16[1,256,2048]{2,1,0:T(8,128)(2,1)} %param.30) | copy-start | bytes 3145732
  1.8 9.0 %copy-start.83 = (f32[32]{0:T(128)}, f32[32]{0:T(128)S(1)}, u32[]{:S(2)}) copy-start(f32[32]{0:T(128)S(1)} %fusion.164) | copy-start | bytes 388
  3.1 4.8 %copy-start.70 = (s32[32]{0:T(128)}, s32[32]{0:T(128)S(1)}, u32[]{:S(2)}) copy-start(s32[32]{0:T(128)S(1)} %get-tuple-element.59) | copy-start | bytes 388
  8.4 14.3 %copy-start.54 = (s32[2,2,1,32,2]{3,4,2,1,0:T(2,128)S(1)}, s32[2,2,1,32,2]{3,4,2,1,0:T(2,128)}, u32[]{:S(2)}) copy-start(s32[2,2,1,32,2]{3,4,2,1,0:T(2,128)} %param.24) | copy-start | bytes 3076
  8.4 16.0 %copy-start.19 = (bf16[1,32,2048]{2,1,0:T(8,128)(2,1)S(1)}, bf16[1,32,2048]{2,1,0:T(8,128)(2,1)}, u32[]{:S(2)}) copy-start(bf16[1,32,2048]{2,1,0:T(8,128)(2,1)} %param.22) | copy-start | bytes 393220
  9.6 15.0 %copy-start.11 = (bf16[1,32,2048]{2,1,0:T(8,128)(2,1)S(1)}, bf16[1,32,2048]{2,1,0:T(8,128)(2,1)}, u32[]{:S(2)}) copy-start(bf16[1,32,2048]{2,1,0:T(8,128)(2,1)} %param.19) | copy-start | bytes 393220
  9.6 15.1 %copy-start.29 = (f32[1,2048]{1,0:T(1,128)S(1)}, f32[1,2048]{1,0:T(1,128)}, u32[]{:S(2)}) copy-start(f32[1,2048]{1,0:T(1,128)} %param.26) | copy-start | bytes 24580
  10.8 27.5 %all-to-all-start.1 = ((bf16[32,8,2048]{2,1,0:T(8,128)(2,1)}), bf16[32,8,2048]{2,1,0:T(8,128)(2,1)S(1)}, u32[]{:S(2)}, u32[]{:S(2)}) async-start(bf16[32,8,2048]{2,1,0:T(8,128)(2,1)} %bitcast.14), calls=%async_computation.1 | async-start | bytes 2097152 | tf_op jit(solution)/shard_map/all_to_all | solution.py:104
  23.3 22.1 %copy-start.58 = (s32[32,2]{0,1:T(2,128)}, s32[32,2]{0,1:T(2,128)S(1)}, u32[]{:S(2)}) copy-start(s32[32,2]{0,1:T(2,128)S(1)} %get-tuple-element.28) | copy-start | bytes 772
  24.6 23.0 %copy-start.9 = (bf16[2,1,32,2048]{3,2,1,0:T(8,128)(2,1)S(1)}, bf16[2,1,32,2048]{3,2,1,0:T(8,128)(2,1)}, u32[]{:S(2)}) copy-start(bf16[2,1,32,2048]{3,2,1,0:T(8,128)(2,1)} %param.21) | copy-start | bytes 786436
  24.8 14.7 %copy-start.98 = (f32[32]{0:T(128)}, f32[32]{0:T(128)S(1)}, u32[]{:S(2)}) copy-start(f32[32]{0:T(128)S(1)} %add_rsqrt_fusion.1) | copy-start | bytes 388
  39.4 6.0 %copy-start.61 = (s32[32,2]{0,1:T(2,128)S(1)}, s32[32,2]{0,1:T(2,128)}, u32[]{:S(2)}) copy-start(s32[32,2]{0,1:T(2,128)} %copy-done.60) | copy-start | bytes 772
  39.5 21.4 %all-to-all-start = ((bf16[32,8,2048]{2,1,0:T(8,128)(2,1)}), bf16[32,8,2048]{2,1,0:T(8,128)(2,1)}, u32[]{:S(2)}, u32[]{:S(2)}) async-start(bf16[32,8,2048]{2,1,0:T(8,128)(2,1)} %bitcast.8), calls=%async_computation | async-start | bytes 2097152 | tf_op jit(solution)/shard_map/all_to_all | solution.py:104
  44.0 25.9 %copy-start.5 = (bf16[1,2048,256]{2,1,0:T(8,128)(2,1)S(1)}, bf16[1,2048,256]{2,1,0:T(8,128)(2,1)}, u32[]{:S(2)}) copy-start(bf16[1,2048,256]{2,1,0:T(8,128)(2,1)} %param.29) | copy-start | bytes 3145732
  62.1 20.9 %all-to-all-start.7 = ((bf16[32,8,2048]{2,1,0:T(8,128)(2,1)}), bf16[32,8,2048]{2,1,0:T(8,128)(2,1)S(1)}, u32[]{:S(2)}, u32[]{:S(2)}) async-start(bf16[32,8,2048]{2,1,0:T(8,128)(2,1)} %bitcast.50), calls=%async_computation.7 | async-start | bytes 2097152 | tf_op jit(solution)/shard_map/all_to_all | solution.py:104
  77.4 11.8 %copy-start.53 = (s32[32,2,1]{1,0,2:T(8,128)S(1)}, s32[32,2,1]{1,0,2:T(8,128)}, u32[]{:S(2)}) copy-start(s32[32,2,1]{1,0,2:T(8,128)} %copy.243) | copy-start | bytes 772
  85.2 10.8 %all-to-all-start.9 = ((bf16[32,1,8]{2,1,0:T(2,128)(2,1)}), bf16[32,1,8]{2,1,0:T(2,128)(2,1)S(1)}, u32[]{:S(2)}, u32[]{:S(2)}) async-start(bf16[32,1,8]{2,1,0:T(2,128)(2,1)} %convert_element_type.401), calls=%async_computation.9 | async-start | bytes 32768 | tf_op jit(solution)/shard_map/all_to_all | solution.py:107
  99.8 11.1 %all-to-all-start.6 = ((bf16[32,1,8]{2,1,0:T(2,128)(2,1)}), bf16[32,1,8]{2,1,0:T(2,128)(2,1)S(1)}, u32[]{:S(2)}, u32[]{:S(2)}) async-start(bf16[32,1,8]{2,1,0:T(2,128)(2,1)} %copy.246), calls=%async_computation.6 | async-start | bytes 32768 | tf_op jit(solution)/shard_map/all_to_all | solution.py:104
  104.0 11.8 %copy-start.66 = (s32[32]{0:T(128)S(1)}, s32[32]{0:T(128)}, u32[]{:S(2)}) copy-start(s32[32]{0:T(128)} %get-tuple-element.60) | copy-start | bytes 388
  104.0 85.1 %copy-start.72 = (s32[1,1,1,32,2]{3,4,2,1,0:T(2,128)S(1)}, s32[1,1,1,32,2]{3,4,2,1,0:T(2,128)}, u32[]{:S(2)}) copy-start(s32[1,1,1,32,2]{3,4,2,1,0:T(2,128)} %get-tuple-element.42) | copy-start | bytes 772
  104.0 90.1 %copy-start.62 = (s32[32,2]{0,1:T(2,128)S(1)}, s32[32,2]{0,1:T(2,128)}, u32[]{:S(2)}) copy-start(s32[32,2]{0,1:T(2,128)} %get-tuple-element.56) | copy-start | bytes 772
  111.6 88.2 %all-to-all-start.2 = ((bf16[32,8,2048]{2,1,0:T(8,128)(2,1)}), bf16[32,8,2048]{2,1,0:T(8,128)(2,1)S(1)}, u32[]{:S(2)}, u32[]{:S(2)}) async-start(bf16[32,8,2048]{2,1,0:T(8,128)(2,1)} %slice_bitcast_fusion.1), calls=%async_computation.2 | async-start | bytes 2097152 | tf_op jit(solution)/shard_map/all_to_all | solution.py:107
  199.7 5.2 %copy-start.86 = (s32[64]{0:T(128)S(1)}, s32[64]{0:T(128)}, u32[]{:S(2)}) copy-start(s32[64]{0:T(128)} %copy-done.85) | copy-start | bytes 772
  199.7 5.2 %copy-start.100 = (s32[64,1]{0,1:T(1,128)S(1)}, s32[64,1]{0,1:T(1,128)}, u32[]{:S(2)}) copy-start(s32[64,1]{0,1:T(1,128)} %mul.452) | copy-start | bytes 772
  199.7 5.8 %copy-start.88 = (pred[32,2]{0,1:T(4,128)(4,1)S(1)}, pred[32,2]{0,1:T(4,128)(4,1)}, u32[]{:S(2)}) copy-start(pred[32,2]{0,1:T(4,128)(4,1)} %get-tuple-element.34) | copy-start | bytes 196
  199.7 6.5 %copy-start.80 = (f32[32,2]{0,1:T(2,128)S(1)}, f32[32,2]{0,1:T(2,128)}, u32[]{:S(2)}) copy-start(f32[32,2]{0,1:T(2,128)} %get-tuple-element.52) | copy-start | bytes 772
  199.7 7.1 %copy-start.75 = (s32[32,2]{0,1:T(2,128)S(1)}, s32[32,2]{0,1:T(2,128)}, u32[]{:S(2)}) copy-start(s32[32,2]{0,1:T(2,128)} %get-tuple-element.40) | copy-start | bytes 772
  199.7 7.1 %copy-start.82 = (f32[32,2]{0,1:T(2,128)S(1)}, f32[32,2]{0,1:T(2,128)}, u32[]{:S(2)}) copy-start(f32[32,2]{0,1:T(2,128)} %get-tuple-element.33) | copy-start | bytes 772
  199.7 21.5 %all-to-all-start.8 = ((bf16[32,8,2048]{2,1,0:T(8,128)(2,1)}), bf16[32,8,2048]{2,1,0:T(8,128)(2,1)}, u32[]{:S(2)}, u32[]{:S(2)}) async-start(bf16[32,8,2048]{2,1,0:T(8,128)(2,1)} %fusion.3), calls=%async_computation.8 | async-start | bytes 2097152 | tf_op jit(solution)/shard_map/all_to_all | solution.py:107
  209.8 22.1 %copy-start.10 = (f32[32,2048]{1,0:T(8,128)}, f32[32,2048]{1,0:T(8,128)S(1)}, u32[]{:S(2)}) copy-start(f32[32,2048]{1,0:T(8,128)S(1)} %fusion.47) | copy-start | bytes 786436
  226.6 50.0 %copy-start.92 = (f32[32]{0:T(128)}, f32[32]{0:T(128)S(1)}, u32[]{:S(2)}) copy-start(f32[32]{0:T(128)S(1)} %fusion.165) | copy-start | bytes 388
  226.6 7.7 %copy-start.89 = (f32[2]{0:T(128)S(1)}, f32[2]{0:T(128)}, u32[]{:S(2)}) copy-start(f32[2]{0:T(128)} %psum.7) | copy-start | bytes 28
  226.6 8.3 %copy-start.76 = (s32[32,2]{0,1:T(2,128)S(1)}, s32[32,2]{0,1:T(2,128)}, u32[]{:S(2)}) copy-start(s32[32,2]{0,1:T(2,128)} %get-tuple-element.75) | copy-start | bytes 772
  226.6 8.5 %copy-start.59 = (s32[32,2]{0,1:T(2,128)S(1)}, s32[32,2]{0,1:T(2,128)}, u32[]{:S(2)}) copy-start(s32[32,2]{0,1:T(2,128)} %copy-done.58) | copy-start | bytes 772
  226.6 8.5 %copy-start.99 = (pred[32,2]{0,1:T(4,128)(4,1)S(1)}, pred[32,2]{0,1:T(4,128)(4,1)}, u32[]{:S(2)}) copy-start(pred[32,2]{0,1:T(4,128)(4,1)} %iota_compare_fusion.11) | copy-start | bytes 196
  226.9 10.3 %copy-start.34 = (bf16[1,32,2048]{2,1,0:T(8,128)(2,1)S(1)}, bf16[1,32,2048]{2,1,0:T(8,128)(2,1)}, u32[]{:S(2)}) copy-start(bf16[1,32,2048]{2,1,0:T(8,128)(2,1)} %param.20) | copy-start | bytes 393220
  228.0 20.9 %all-to-all-start.4 = ((bf16[32,8,2048]{2,1,0:T(8,128)(2,1)}), bf16[32,8,2048]{2,1,0:T(8,128)(2,1)S(1)}, u32[]{:S(2)}, u32[]{:S(2)}) async-start(bf16[32,8,2048]{2,1,0:T(8,128)(2,1)} %bitcast.34), calls=%async_computation.4 | async-start | bytes 2097152 | tf_op jit(solution)/shard_map/all_to_all | solution.py:104
  232.7 4.5 %collective-permute-start = (bf16[32,2048]{1,0:T(8,128)(2,1)}, bf16[32,2048]{1,0:T(8,128)(2,1)S(1)}, u32[]{:S(2)}, u32[]{:S(2)}) collective-permute-start(bf16[32,2048]{1,0:T(8,128)(2,1)} %fusion.74), channel_id=1, source_target_pairs={{0,32},{32,64},{64,96},{96,128},{128,160},{160,192},{192,224},{224... | collective-permute-start | bytes 393224 | tf_op jit(solution)/shard_map/ppermute | solution.py:21
  235.2 19.3 %copy-start.95 = (f32[32]{0:T(128)S(1)}, f32[32]{0:T(128)}, u32[]{:S(2)}) copy-start(f32[32]{0:T(128)} %copy-done.94) | copy-start | bytes 388
  235.3 19.3 %copy-start.20 = (bf16[1,32,2048]{2,1,0:T(8,128)(2,1)S(1)}, bf16[1,32,2048]{2,1,0:T(8,128)(2,1)}, u32[]{:S(2)}) copy-start(bf16[1,32,2048]{2,1,0:T(8,128)(2,1)} %param.22) | copy-start | bytes 393220
  235.3 19.3 %copy-start.84 = (f32[32]{0:T(128)S(1)}, f32[32]{0:T(128)}, u32[]{:S(2)}) copy-start(f32[32]{0:T(128)} %copy-done.83) | copy-start | bytes 388
  238.3 19.8 %copy-start.79 = (s32[32,2,1]{0,1,2:T(2,128)S(1)}, s32[32,2,1]{0,1,2:T(2,128)}, u32[]{:S(2)}) copy-start(s32[32,2,1]{0,1,2:T(2,128)} %get-tuple-element.48) | copy-start | bytes 772
  238.3 20.0 %copy-start.73 = (f32[32,2]{0,1:T(2,128)S(1)}, f32[32,2]{0,1:T(2,128)}, u32[]{:S(2)}) copy-start(f32[32,2]{0,1:T(2,128)} %get-tuple-element.63) | copy-start | bytes 772
  238.3 20.7 %copy-start.78 = (s32[32,2,1]{0,1,2:T(2,128)S(1)}, s32[32,2,1]{0,1,2:T(2,128)}, u32[]{:S(2)}) copy-start(s32[32,2,1]{0,1,2:T(2,128)} %get-tuple-element.51) | copy-start | bytes 772
  238.3 20.9 %copy-start.87 = (pred[32,2]{0,1:T(4,128)(4,1)S(1)}, pred[32,2]{0,1:T(4,128)(4,1)}, u32[]{:S(2)}) copy-start(pred[32,2]{0,1:T(4,128)(4,1)} %get-tuple-element.27) | copy-start | bytes 196
  238.4 21.6 %copy-start.77 = (s32[32,2]{0,1:T(2,128)S(1)}, s32[32,2]{0,1:T(2,128)}, u32[]{:S(2)}) copy-start(s32[32,2]{0,1:T(2,128)} %get-tuple-element.55) | copy-start | bytes 772
  238.4 23.1 %copy-start.21 = (bf16[1,32,2048]{2,1,0:T(8,128)(2,1)S(1)}, bf16[1,32,2048]{2,1,0:T(8,128)(2,1)}, u32[]{:S(2)}) copy-start(bf16[1,32,2048]{2,1,0:T(8,128)(2,1)} %param.23) | copy-start | bytes 393220
  248.9 9.2 %copy-start.15 = (bf16[32,8,2048]{2,1,0:T(8,128)(2,1)}, bf16[32,8,2048]{2,1,0:T(8,128)(2,1)S(1)}, u32[]{:S(2)}) copy-start(bf16[32,8,2048]{2,1,0:T(8,128)(2,1)S(1)} %all-to-all-done.4) | copy-start | bytes 3145732
  250.1 21.4 %all-to-all-start.3 = ((bf16[32,8,2048]{2,1,0:T(8,128)(2,1)}), bf16[32,8,2048]{2,1,0:T(8,128)(2,1)}, u32[]{:S(2)}, u32[]{:S(2)}) async-start(bf16[32,8,2048]{2,1,0:T(8,128)(2,1)} %bitcast.28), calls=%async_computation.3 | async-start | bytes 2097152 | tf_op jit(solution)/shard_map/all_to_all | solution.py:104
  254.7 6.0 %copy-start.23 = (bf16[32,2048]{1,0:T(8,128)(2,1)}, bf16[32,2048]{1,0:T(8,128)(2,1)S(1)}, u32[]{:S(2)}) copy-start(bf16[32,2048]{1,0:T(8,128)(2,1)S(1)} %fusion.83) | copy-start | bytes 393220
  254.7 6.7 %collective-permute-start.1 = (bf16[32,2048]{1,0:T(8,128)(2,1)S(1)}, bf16[32,2048]{1,0:T(8,128)(2,1)S(1)}, u32[]{:S(2)}, u32[]{:S(2)}) collective-permute-start(bf16[32,2048]{1,0:T(8,128)(2,1)S(1)} %fusion.83), channel_id=1, source_target_pairs={{32,0},{64,32},{96,64},{128,96},{160,128},{192,160},{224,192},{256... | collective-permute-start | bytes 393224 | tf_op jit(solution)/shard_map/ppermute | solution.py:21
  261.5 11.2 %copy-start.25 = (bf16[32,2048]{1,0:T(8,128)(2,1)}, bf16[32,2048]{1,0:T(8,128)(2,1)S(1)}, u32[]{:S(2)}) copy-start(bf16[32,2048]{1,0:T(8,128)(2,1)S(1)} %collective-permute-done.1) | copy-start | bytes 393220
  272.6 20.9 %all-to-all-start.11 = ((bf16[32,8,2048]{2,1,0:T(8,128)(2,1)}), bf16[32,8,2048]{2,1,0:T(8,128)(2,1)S(1)}, u32[]{:S(2)}, u32[]{:S(2)}) async-start(bf16[32,8,2048]{2,1,0:T(8,128)(2,1)} %bitcast.67), calls=%async_computation.11 | async-start | bytes 2097152 | tf_op jit(solution)/shard_map/all_to_all | solution.py:104
  287.4 12.4 %copy-start.13 = (bf16[32,2048]{1,0:T(8,128)(2,1)S(1)}, bf16[32,2048]{1,0:T(8,128)(2,1)}, u32[]{:S(2)}) copy-start(bf16[32,2048]{1,0:T(8,128)(2,1)} %copy-done.12) | copy-start | bytes 393220
  287.4 12.4 %copy-start.31 = (f32[1,2048]{1,0:T(1,128)S(1)}, f32[1,2048]{1,0:T(1,128)}, u32[]{:S(2)}) copy-start(f32[1,2048]{1,0:T(1,128)} %param.26) | copy-start | bytes 24580
  287.4 12.4 %copy-start.36 = (bf16[1,2048,8]{1,2,0:T(8,128)(2,1)S(1)}, bf16[1,2048,8]{1,2,0:T(8,128)(2,1)}, u32[]{:S(2)}) copy-start(bf16[1,2048,8]{1,2,0:T(8,128)(2,1)} %param.27) | copy-start | bytes 98308
  287.4 12.4 %copy-start.97 = (f32[32]{0:T(128)S(1)}, f32[32]{0:T(128)}, u32[]{:S(2)}) copy-start(f32[32]{0:T(128)} %copy-done.96) | copy-start | bytes 388
  295.8 10.9 %all-to-all-start.13 = ((bf16[32,1,8]{2,1,0:T(2,128)(2,1)}), bf16[32,1,8]{2,1,0:T(2,128)(2,1)S(1)}, u32[]{:S(2)}, u32[]{:S(2)}) async-start(bf16[32,1,8]{2,1,0:T(2,128)(2,1)} %convert_element_type.402), calls=%async_computation.13 | async-start | bytes 32768 | tf_op jit(solution)/shard_map/all_to_all | solution.py:107
  300.0 6.8 %copy-start.28 = (s32[1024]{0:T(1024)S(1)}, s32[1024]{0:T(1024)}, u32[]{:S(2)}) copy-start(s32[1024]{0:T(1024)} %pad_clamp_fusion) | copy-start | bytes 12292
  310.5 11.4 %all-to-all-start.10 = ((bf16[32,1,8]{2,1,0:T(2,128)(2,1)}), bf16[32,1,8]{2,1,0:T(2,128)(2,1)S(1)}, u32[]{:S(2)}, u32[]{:S(2)}) async-start(bf16[32,1,8]{2,1,0:T(2,128)(2,1)} %copy.257), calls=%async_computation.10 | async-start | bytes 32768 | tf_op jit(solution)/shard_map/all_to_all | solution.py:104
  314.9 15.0 %copy-start.74 = (s32[32,2]{0,1:T(2,128)S(1)}, s32[32,2]{0,1:T(2,128)}, u32[]{:S(2)}) copy-start(s32[32,2]{0,1:T(2,128)} %get-tuple-element.39) | copy-start | bytes 772
  322.5 21.2 %all-to-all-start.5 = ((bf16[32,8,2048]{2,1,0:T(8,128)(2,1)}), bf16[32,8,2048]{2,1,0:T(8,128)(2,1)S(1)}, u32[]{:S(2)}, u32[]{:S(2)}) async-start(bf16[32,8,2048]{2,1,0:T(8,128)(2,1)} %slice_bitcast_fusion), calls=%async_computation.5 | async-start | bytes 2097152 | tf_op jit(solution)/shard_map/all_to_all | solution.py:107
  334.8 13.6 %copy-start.46 = (s32[1024]{0:T(1024)S(1)}, s32[1024]{0:T(1024)}, u32[]{:S(2)}) copy-start(s32[1024]{0:T(1024)} %pad_clamp_fusion.2) | copy-start | bytes 12292
  343.8 21.4 %all-to-all-start.12 = ((bf16[32,8,2048]{2,1,0:T(8,128)(2,1)}), bf16[32,8,2048]{2,1,0:T(8,128)(2,1)}, u32[]{:S(2)}, u32[]{:S(2)}) async-start(bf16[32,8,2048]{2,1,0:T(8,128)(2,1)} %fusion.2), calls=%async_computation.12 | async-start | bytes 2097152 | tf_op jit(solution)/shard_map/all_to_all | solution.py:107
  (55 other events, 102.4 us)
where the time goes:
time: 374 us; the launch traced here: 372 us
  waiting for transfers between devices  113 us (30%)
  blocking collectives  71.3 us (19%)
  starting transfers between devices  68 us (18%)
  local copies, waits for them, and re-layouts  49.2 us (13%)
  other arithmetic  39.3 us (11%)
  matrix products  25.7 us (7%)
  between operations  5.49 us (1%)
    psum x1, blocking collectives, on_device(): lax.psum(jnp.sum(counts[0, :, 0], axis=-1).astype(jnp.float32), 'expert')  71.3 us
    all_to_all x8, waiting for transfers between devices, route_rows(): lax.all_to_all(shortened(outgoing), 'expert', split_axis=0, concat_axis=0...  66.3 us
    all_to_all x6, waiting for transfers between devices, route_rows(): lax.all_to_all(shortened(work(*received)), 'expert', split_axis=0, concat...  44 us
    all_to_all x8, starting transfers between devices, route_rows(): lax.all_to_all(shortened(outgoing), 'expert', split_axis=0, concat_axis=0...  39.7 us
    all_to_all x6, starting transfers between devices, route_rows(): lax.all_to_all(shortened(work(*received)), 'expert', split_axis=0, concat...  25.5 us
  transfers between devices with their start and end apart: 16, of which 15 were waited for; matrix products, arithmetic and copies ran while one was open for 19% of the time, Pallas kernels for 0%

commit v1 on v0

--- a/solution.py
+++ b/solution.py
@@ -147,7 +147,9 @@
     gate_cols = w_gate[0]
     up_cols = w_up[0]
     down_rows = w_down[0]
-    totals = lax.psum(jnp.sum(counts[0, :, 0], axis=-1).astype(jnp.float32), "expert")
+    totals = jnp.sum(
+        lax.all_gather(jnp.sum(counts[0, :, 0], axis=-1).astype(jnp.float32), "expert"), axis=0
+    )
     weight = lam[0]
     forward_x = section_in[0]
     cotangent = grad_in[0]

time: 374 us -> 374 us (level)
    psum x1 -> x0, blocking collectives: 71.3 us -> none  [on_device(): lax.psum(jnp.sum(counts[0, :, 0], axis=-1).astype(jnp.float32), 'expert')]
    unnamed x0 -> x1, blocking collectives: none -> 68.8 us
  transfers between devices with their start and end apart: 16 -> 16, of which waited for: 15 -> 15; matrix products, arithmetic and copies ran while one was open for 19% -> 20% of each run, Pallas kernels for 0% -> 0%
where the time goes in v1:
time: 374 us; the launch traced here: 372 us
  waiting for transfers between devices  113 us (30%)
  blocking collectives  68.8 us (18%)
  starting transfers between devices  68 us (18%)
  local copies, waits for them, and re-layouts  52.4 us (14%)
  other arithmetic  40 us (11%)
  matrix products  24.1 us (6%)
  between operations  6.02 us (2%)
    unnamed x1, blocking collectives  68.8 us
    all_to_all x8, waiting for transfers between devices, route_rows(): lax.all_to_all(shortened(outgoing), 'expert', split_axis=0, concat_axis=0...  66.5 us
    all_to_all x6, waiting for transfers between devices, route_rows(): lax.all_to_all(shortened(work(*received)), 'expert', split_axis=0, concat...  43.3 us
    all_to_all x8, starting transfers between devices, route_rows(): lax.all_to_all(shortened(outgoing), 'expert', split_axis=0, concat_axis=0...  39.6 us
    all_to_all x6, starting transfers between devices, route_rows(): lax.all_to_all(shortened(work(*received)), 'expert', split_axis=0, concat...  25.5 us
  transfers between devices with their start and end apart: 16, of which 15 were waited for; matrix products, arithmetic and copies ran while one was open for 20% of the time, Pallas kernels for 0%

profile of v1, /device:TPU:1, one launch (start us, length us, event | category | flops | bytes accessed | tf_op | source)
XLA Modules:
  0.0 371.9 jit_solution(1886799311254372221)
XLA Ops:
  0.6 1.1 fusion.59
  1.8 1.2 slice_bitcast_fusion.3
  3.0 1.3 slice_bitcast_fusion.6
  6.5 1.3 compare_select_fusion.2
  8.3 1.2 fusion.5
  10.7 10.5 %all-to-all-start.1 = ((bf16[32,8,2048]{2,1,0:T(8,128)(2,1)}), bf16[32,8,2048]{2,1,0:T(8,128)(2,1)S(1)}, u32[]{:S(2)}, u32[]{:S(2)}) async-start(bf16[32,8,2048]{2,1,0:T(8,128)(2,1)} %bitcast.14), calls=%async_computation.1 | async-start | bytes 2097152 | tf_op jit(solution)/shard_map/all_to_all | solution.py:104
  25.6 12.6 %all-to-all-done.1 = bf16[32,8,2048]{2,1,0:T(8,128)(2,1)S(1)} async-done(((bf16[32,8,2048]{2,1,0:T(8,128)(2,1)}), bf16[32,8,2048]{2,1,0:T(8,128)(2,1)S(1)}, u32[]{:S(2)}, u32[]{:S(2)}) %all-to-all-start.1) | async-done | bytes 1048608 | tf_op jit(solution)/shard_map/all_to_all | solution.py:104
  38.2 1.2 broadcast_in_dim.59
  39.4 4.4 %all-to-all-start = ((bf16[32,8,2048]{2,1,0:T(8,128)(2,1)}), bf16[32,8,2048]{2,1,0:T(8,128)(2,1)}, u32[]{:S(2)}, u32[]{:S(2)}) async-start(bf16[32,8,2048]{2,1,0:T(8,128)(2,1)} %bitcast.8), calls=%async_computation | async-start | bytes 2097152 | tf_op jit(solution)/shard_map/all_to_all | solution.py:104
  46.2 14.6 %all-to-all-done = bf16[32,8,2048]{2,1,0:T(8,128)(2,1)} async-done(((bf16[32,8,2048]{2,1,0:T(8,128)(2,1)}), bf16[32,8,2048]{2,1,0:T(8,128)(2,1)}, u32[]{:S(2)}, u32[]{:S(2)}) %all-to-all-start) | async-done | bytes 1048608 | tf_op jit(solution)/shard_map/all_to_all | solution.py:104
  61.9 3.9 %all-to-all-start.7 = ((bf16[32,8,2048]{2,1,0:T(8,128)(2,1)}), bf16[32,8,2048]{2,1,0:T(8,128)(2,1)S(1)}, u32[]{:S(2)}, u32[]{:S(2)}) async-start(bf16[32,8,2048]{2,1,0:T(8,128)(2,1)} %bitcast.50), calls=%async_computation.7 | async-start | bytes 2097152 | tf_op jit(solution)/shard_map/all_to_all | solution.py:104
  69.6 1.4 copy.222
  71.8 2.4 fusion.20
  74.2 2.9 divide_multiply_fusion.1
  77.2 2.1 convolution_convert_fusion.1
  79.3 3.5 all-to-all-done.7
  82.8 1.6 fusion.14
  85.1 4.0 %all-to-all-start.9 = ((bf16[32,1,8]{2,1,0:T(2,128)(2,1)}), bf16[32,1,8]{2,1,0:T(2,128)(2,1)S(1)}, u32[]{:S(2)}, u32[]{:S(2)}) async-start(bf16[32,1,8]{2,1,0:T(2,128)(2,1)} %convert_element_type.412), calls=%async_computation.9 | async-start | bytes 32768 | tf_op jit(solution)/shard_map/all_to_all | solution.py:107
  90.0 1.3 dynamic-slice
  91.8 4.1 %all-to-all-done.9 = bf16[32,1,8]{2,1,0:T(2,128)(2,1)S(1)} async-done(((bf16[32,1,8]{2,1,0:T(2,128)(2,1)}), bf16[32,1,8]{2,1,0:T(2,128)(2,1)S(1)}, u32[]{:S(2)}, u32[]{:S(2)}) %all-to-all-start.9) | async-done | bytes 544 | tf_op jit(solution)/shard_map/all_to_all | solution.py:107
  99.7 4.1 %all-to-all-start.6 = ((bf16[32,1,8]{2,1,0:T(2,128)(2,1)}), bf16[32,1,8]{2,1,0:T(2,128)(2,1)S(1)}, u32[]{:S(2)}, u32[]{:S(2)}) async-start(bf16[32,1,8]{2,1,0:T(2,128)(2,1)} %copy.246), calls=%async_computation.6 | async-start | bytes 32768 | tf_op jit(solution)/shard_map/all_to_all | solution.py:104
  103.9 2.3 slice_bitcast_fusion.1
  106.2 4.6 %all-to-all-done.6 = bf16[32,1,8]{2,1,0:T(2,128)(2,1)S(1)} async-done(((bf16[32,1,8]{2,1,0:T(2,128)(2,1)}), bf16[32,1,8]{2,1,0:T(2,128)(2,1)S(1)}, u32[]{:S(2)}, u32[]{:S(2)}) %all-to-all-start.6) | async-done | bytes 544 | tf_op jit(solution)/shard_map/all_to_all | solution.py:104
  111.5 4.2 %all-to-all-start.2 = ((bf16[32,8,2048]{2,1,0:T(8,128)(2,1)}), bf16[32,8,2048]{2,1,0:T(8,128)(2,1)S(1)}, u32[]{:S(2)}, u32[]{:S(2)}) async-start(bf16[32,8,2048]{2,1,0:T(8,128)(2,1)} %slice_bitcast_fusion.1), calls=%async_computation.2 | async-start | bytes 2097152 | tf_op jit(solution)/shard_map/all_to_all | solution.py:107
  116.3 1.3 convert_dynamic-update-slice_fusion
  118.3 68.8 %all-reduce = f32[64]{0:T(128)S(1)} all-reduce(f32[64]{0:T(128)} %convert_dynamic-update-slice_fusion), channel_id=2, replica_groups=mesh['section'=16,'expert'=32] {'expert'}, use_global_device_ids=true, to_apply=%add | all-reduce | flops 64 | bytes 512
  187.8 1.3 reduce_sum.334
  189.8 1.4 mul.452
  191.9 1.3 copy.230
  194.1 1.5 convert_reduce_fusion.4
  198.2 1.4 fusion.3
  199.7 4.7 %all-to-all-start.8 = ((bf16[32,8,2048]{2,1,0:T(8,128)(2,1)}), bf16[32,8,2048]{2,1,0:T(8,128)(2,1)}, u32[]{:S(2)}, u32[]{:S(2)}) async-start(bf16[32,8,2048]{2,1,0:T(8,128)(2,1)} %fusion.3), calls=%async_computation.8 | async-start | bytes 2097152 | tf_op jit(solution)/shard_map/all_to_all | solution.py:107
  208.1 1.7 fusion.47
  209.8 11.4 %all-to-all-done.8 = bf16[32,8,2048]{2,1,0:T(8,128)(2,1)} async-done(((bf16[32,8,2048]{2,1,0:T(8,128)(2,1)}), bf16[32,8,2048]{2,1,0:T(8,128)(2,1)}, u32[]{:S(2)}, u32[]{:S(2)}) %all-to-all-start.8) | async-done | bytes 1048608 | tf_op jit(solution)/shard_map/all_to_all | solution.py:107
  221.2 1.4 convert_reduce_fusion.1
  223.8 1.7 fusion.45
  228.0 3.9 %all-to-all-start.4 = ((bf16[32,8,2048]{2,1,0:T(8,128)(2,1)}), bf16[32,8,2048]{2,1,0:T(8,128)(2,1)S(1)}, u32[]{:S(2)}, u32[]{:S(2)}) async-start(bf16[32,8,2048]{2,1,0:T(8,128)(2,1)} %bitcast.34), calls=%async_computation.4 | async-start | bytes 2097152 | tf_op jit(solution)/shard_map/all_to_all | solution.py:104
  232.6 1.6 collective-permute-start
  235.1 2.0 collective-permute-done
  238.3 10.5 %all-to-all-done.4 = bf16[32,8,2048]{2,1,0:T(8,128)(2,1)S(1)} async-done(((bf16[32,8,2048]{2,1,0:T(8,128)(2,1)}), bf16[32,8,2048]{2,1,0:T(8,128)(2,1)S(1)}, u32[]{:S(2)}, u32[]{:S(2)}) %all-to-all-start.4) | async-done | bytes 1048608 | tf_op jit(solution)/shard_map/all_to_all | solution.py:104
  248.8 1.2 broadcast_in_dim.63
  250.0 4.5 %all-to-all-start.3 = ((bf16[32,8,2048]{2,1,0:T(8,128)(2,1)}), bf16[32,8,2048]{2,1,0:T(8,128)(2,1)}, u32[]{:S(2)}, u32[]{:S(2)}) async-start(bf16[32,8,2048]{2,1,0:T(8,128)(2,1)} %bitcast.28), calls=%async_computation.3 | async-start | bytes 2097152 | tf_op jit(solution)/shard_map/all_to_all | solution.py:104
  254.7 1.3 collective-permute-start.1
  261.6 9.8 %all-to-all-done.3 = bf16[32,8,2048]{2,1,0:T(8,128)(2,1)} async-done(((bf16[32,8,2048]{2,1,0:T(8,128)(2,1)}), bf16[32,8,2048]{2,1,0:T(8,128)(2,1)}, u32[]{:S(2)}, u32[]{:S(2)}) %all-to-all-start.3) | async-done | bytes 1048608 | tf_op jit(solution)/shard_map/all_to_all | solution.py:104
  272.6 3.9 %all-to-all-start.11 = ((bf16[32,8,2048]{2,1,0:T(8,128)(2,1)}), bf16[32,8,2048]{2,1,0:T(8,128)(2,1)S(1)}, u32[]{:S(2)}, u32[]{:S(2)}) async-start(bf16[32,8,2048]{2,1,0:T(8,128)(2,1)} %bitcast.67), calls=%async_computation.11 | async-start | bytes 2097152 | tf_op jit(solution)/shard_map/all_to_all | solution.py:104
  279.0 2.4 fusion.18
  281.5 2.9 divide_multiply_fusion
  285.2 2.1 convolution_convert_fusion
  287.3 6.1 %all-to-all-done.11 = bf16[32,8,2048]{2,1,0:T(8,128)(2,1)S(1)} async-done(((bf16[32,8,2048]{2,1,0:T(8,128)(2,1)}), bf16[32,8,2048]{2,1,0:T(8,128)(2,1)S(1)}, u32[]{:S(2)}, u32[]{:S(2)}) %all-to-all-start.11) | async-done | bytes 1048608 | tf_op jit(solution)/shard_map/all_to_all | solution.py:104
  293.4 1.6 fusion.17
  295.7 4.0 %all-to-all-start.13 = ((bf16[32,1,8]{2,1,0:T(2,128)(2,1)}), bf16[32,1,8]{2,1,0:T(2,128)(2,1)S(1)}, u32[]{:S(2)}, u32[]{:S(2)}) async-start(bf16[32,1,8]{2,1,0:T(2,128)(2,1)} %convert_element_type.413), calls=%async_computation.13 | async-start | bytes 32768 | tf_op jit(solution)/shard_map/all_to_all | solution.py:107
  300.9 5.7 %all-to-all-done.13 = bf16[32,1,8]{2,1,0:T(2,128)(2,1)S(1)} async-done(((bf16[32,1,8]{2,1,0:T(2,128)(2,1)}), bf16[32,1,8]{2,1,0:T(2,128)(2,1)S(1)}, u32[]{:S(2)}, u32[]{:S(2)}) %all-to-all-start.13) | async-done | bytes 544 | tf_op jit(solution)/shard_map/all_to_all | solution.py:107
  310.4 4.3 %all-to-all-start.10 = ((bf16[32,1,8]{2,1,0:T(2,128)(2,1)}), bf16[32,1,8]{2,1,0:T(2,128)(2,1)S(1)}, u32[]{:S(2)}, u32[]{:S(2)}) async-start(bf16[32,1,8]{2,1,0:T(2,128)(2,1)} %copy.257), calls=%async_computation.10 | async-start | bytes 32768 | tf_op jit(solution)/shard_map/all_to_all | solution.py:104
  314.7 2.3 slice_bitcast_fusion
  317.1 4.7 %all-to-all-done.10 = bf16[32,1,8]{2,1,0:T(2,128)(2,1)S(1)} async-done(((bf16[32,1,8]{2,1,0:T(2,128)(2,1)}), bf16[32,1,8]{2,1,0:T(2,128)(2,1)S(1)}, u32[]{:S(2)}, u32[]{:S(2)}) %all-to-all-start.10) | async-done | bytes 544 | tf_op jit(solution)/shard_map/all_to_all | solution.py:104
  322.4 4.2 %all-to-all-start.5 = ((bf16[32,8,2048]{2,1,0:T(8,128)(2,1)}), bf16[32,8,2048]{2,1,0:T(8,128)(2,1)S(1)}, u32[]{:S(2)}, u32[]{:S(2)}) async-start(bf16[32,8,2048]{2,1,0:T(8,128)(2,1)} %slice_bitcast_fusion), calls=%async_computation.5 | async-start | bytes 2097152 | tf_op jit(solution)/shard_map/all_to_all | solution.py:107
  326.6 1.7 fusion.77
  333.3 1.4 fusion.2
  334.7 8.9 %all-to-all-done.5 = bf16[32,8,2048]{2,1,0:T(8,128)(2,1)S(1)} async-done(((bf16[32,8,2048]{2,1,0:T(8,128)(2,1)}), bf16[32,8,2048]{2,1,0:T(8,128)(2,1)S(1)}, u32[]{:S(2)}, u32[]{:S(2)}) %all-to-all-start.5) | async-done | bytes 1048608 | tf_op jit(solution)/shard_map/all_to_all | solution.py:107
  343.6 4.5 %all-to-all-start.12 = ((bf16[32,8,2048]{2,1,0:T(8,128)(2,1)}), bf16[32,8,2048]{2,1,0:T(8,128)(2,1)}, u32[]{:S(2)}, u32[]{:S(2)}) async-start(bf16[32,8,2048]{2,1,0:T(8,128)(2,1)} %fusion.2), calls=%async_computation.12 | async-start | bytes 2097152 | tf_op jit(solution)/shard_map/all_to_all | solution.py:107
  349.4 1.7 fusion.46
  351.9 13.2 %all-to-all-done.12 = bf16[32,8,2048]{2,1,0:T(8,128)(2,1)} async-done(((bf16[32,8,2048]{2,1,0:T(8,128)(2,1)}), bf16[32,8,2048]{2,1,0:T(8,128)(2,1)}, u32[]{:S(2)}, u32[]{:S(2)}) %all-to-all-start.12) | async-done | bytes 1048608 | tf_op jit(solution)/shard_map/all_to_all | solution.py:107
  365.0 1.4 convert_reduce_fusion
  367.6 1.7 fusion.44
  (369 shorter events, 62.2 us)
Async XLA Ops:
  0.6 76.6 %copy-start = (bf16[1,256,2048]{2,1,0:T(8,128)(2,1)S(1)}, bf16[1,256,2048]{2,1,0:T(8,128)(2,1)}, u32[]{:S(2)}) copy-start(bf16[1,256,2048]{2,1,0:T(8,128)(2,1)} %param.30) | copy-start | bytes 3145732
  1.8 44.2 %copy-start.84 = (f32[32]{0:T(128)}, f32[32]{0:T(128)S(1)}, u32[]{:S(2)}) copy-start(f32[32]{0:T(128)S(1)} %fusion.164) | copy-start | bytes 388
  3.0 22.0 %copy-start.67 = (s32[32]{0:T(128)}, s32[32]{0:T(128)S(1)}, u32[]{:S(2)}) copy-start(s32[32]{0:T(128)S(1)} %get-tuple-element.60) | copy-start | bytes 388
  8.3 14.7 %copy-start.19 = (bf16[1,32,2048]{2,1,0:T(8,128)(2,1)S(1)}, bf16[1,32,2048]{2,1,0:T(8,128)(2,1)}, u32[]{:S(2)}) copy-start(bf16[1,32,2048]{2,1,0:T(8,128)(2,1)} %param.22) | copy-start | bytes 393220
  9.6 13.8 %copy-start.55 = (s32[2,2,1,32,2]{3,4,2,1,0:T(2,128)S(1)}, s32[2,2,1,32,2]{3,4,2,1,0:T(2,128)}, u32[]{:S(2)}) copy-start(s32[2,2,1,32,2]{3,4,2,1,0:T(2,128)} %param.24) | copy-start | bytes 3076
  9.6 14.4 %copy-start.11 = (bf16[1,32,2048]{2,1,0:T(8,128)(2,1)S(1)}, bf16[1,32,2048]{2,1,0:T(8,128)(2,1)}, u32[]{:S(2)}) copy-start(bf16[1,32,2048]{2,1,0:T(8,128)(2,1)} %param.19) | copy-start | bytes 393220
  9.6 14.6 %copy-start.30 = (f32[1,2048]{1,0:T(1,128)S(1)}, f32[1,2048]{1,0:T(1,128)}, u32[]{:S(2)}) copy-start(f32[1,2048]{1,0:T(1,128)} %param.26) | copy-start | bytes 24580
  10.7 27.5 %all-to-all-start.1 = ((bf16[32,8,2048]{2,1,0:T(8,128)(2,1)}), bf16[32,8,2048]{2,1,0:T(8,128)(2,1)S(1)}, u32[]{:S(2)}, u32[]{:S(2)}) async-start(bf16[32,8,2048]{2,1,0:T(8,128)(2,1)} %bitcast.14), calls=%async_computation.1 | async-start | bytes 2097152 | tf_op jit(solution)/shard_map/all_to_all | solution.py:104
  23.1 20.7 %copy-start.90 = (s32[2,2,1,32]{3,2,1,0:T(1,128)S(1)}, s32[2,2,1,32]{3,2,1,0:T(1,128)}, u32[]{:S(2)}) copy-start(s32[2,2,1,32]{3,2,1,0:T(1,128)} %param.25) | copy-start | bytes 1540
  23.4 22.4 %copy-start.36 = (bf16[1,2048,8]{1,2,0:T(8,128)(2,1)S(1)}, bf16[1,2048,8]{1,2,0:T(8,128)(2,1)}, u32[]{:S(2)}) copy-start(bf16[1,2048,8]{1,2,0:T(8,128)(2,1)} %param.27) | copy-start | bytes 98308
  23.9 22.1 %copy-start.60 = (s32[32,2]{0,1:T(2,128)}, s32[32,2]{0,1:T(2,128)S(1)}, u32[]{:S(2)}) copy-start(s32[32,2]{0,1:T(2,128)S(1)} %get-tuple-element.28) | copy-start | bytes 772
  24.0 22.0 %copy-start.9 = (bf16[2,1,32,2048]{3,2,1,0:T(8,128)(2,1)S(1)}, bf16[2,1,32,2048]{3,2,1,0:T(8,128)(2,1)}, u32[]{:S(2)}) copy-start(bf16[2,1,32,2048]{3,2,1,0:T(8,128)(2,1)} %param.21) | copy-start | bytes 786436
  38.2 7.0 %copy-start.17 = (bf16[32,8,2048]{2,1,0:T(8,128)(2,1)}, bf16[32,8,2048]{2,1,0:T(8,128)(2,1)S(1)}, u32[]{:S(2)}) copy-start(bf16[32,8,2048]{2,1,0:T(8,128)(2,1)S(1)} %all-to-all-done.1) | copy-start | bytes 3145732
  39.4 21.4 %all-to-all-start = ((bf16[32,8,2048]{2,1,0:T(8,128)(2,1)}), bf16[32,8,2048]{2,1,0:T(8,128)(2,1)}, u32[]{:S(2)}, u32[]{:S(2)}) async-start(bf16[32,8,2048]{2,1,0:T(8,128)(2,1)} %bitcast.8), calls=%async_computation | async-start | bytes 2097152 | tf_op jit(solution)/shard_map/all_to_all | solution.py:104
  61.9 20.9 %all-to-all-start.7 = ((bf16[32,8,2048]{2,1,0:T(8,128)(2,1)}), bf16[32,8,2048]{2,1,0:T(8,128)(2,1)S(1)}, u32[]{:S(2)}, u32[]{:S(2)}) async-start(bf16[32,8,2048]{2,1,0:T(8,128)(2,1)} %bitcast.50), calls=%async_computation.7 | async-start | bytes 2097152 | tf_op jit(solution)/shard_map/all_to_all | solution.py:104
  85.1 10.8 %all-to-all-start.9 = ((bf16[32,1,8]{2,1,0:T(2,128)(2,1)}), bf16[32,1,8]{2,1,0:T(2,128)(2,1)S(1)}, u32[]{:S(2)}, u32[]{:S(2)}) async-start(bf16[32,1,8]{2,1,0:T(2,128)(2,1)} %convert_element_type.412), calls=%async_computation.9 | async-start | bytes 32768 | tf_op jit(solution)/shard_map/all_to_all | solution.py:107
  89.0 7.0 %copy-start.28 = (s32[1024]{0:T(1024)S(1)}, s32[1024]{0:T(1024)}, u32[]{:S(2)}) copy-start(s32[1024]{0:T(1024)} %pad_clamp_fusion.1) | copy-start | bytes 12292
  99.7 11.1 %all-to-all-start.6 = ((bf16[32,1,8]{2,1,0:T(2,128)(2,1)}), bf16[32,1,8]{2,1,0:T(2,128)(2,1)S(1)}, u32[]{:S(2)}, u32[]{:S(2)}) async-start(bf16[32,1,8]{2,1,0:T(2,128)(2,1)} %copy.246), calls=%async_computation.6 | async-start | bytes 32768 | tf_op jit(solution)/shard_map/all_to_all | solution.py:104
  103.9 13.7 %copy-start.74 = (f32[32,2]{0,1:T(2,128)S(1)}, f32[32,2]{0,1:T(2,128)}, u32[]{:S(2)}) copy-start(f32[32,2]{0,1:T(2,128)} %get-tuple-element.65) | copy-start | bytes 772
  103.9 85.2 %copy-start.73 = (s32[1,1,1,32,2]{3,4,2,1,0:T(2,128)S(1)}, s32[1,1,1,32,2]{3,4,2,1,0:T(2,128)}, u32[]{:S(2)}) copy-start(s32[1,1,1,32,2]{3,4,2,1,0:T(2,128)} %get-tuple-element.42) | copy-start | bytes 772
  103.9 90.2 %copy-start.62 = (s32[32,2]{0,1:T(2,128)S(1)}, s32[32,2]{0,1:T(2,128)}, u32[]{:S(2)}) copy-start(s32[32,2]{0,1:T(2,128)} %get-tuple-element.56) | copy-start | bytes 772
  111.5 88.3 %all-to-all-start.2 = ((bf16[32,8,2048]{2,1,0:T(8,128)(2,1)}), bf16[32,8,2048]{2,1,0:T(8,128)(2,1)S(1)}, u32[]{:S(2)}, u32[]{:S(2)}) async-start(bf16[32,8,2048]{2,1,0:T(8,128)(2,1)} %slice_bitcast_fusion.1), calls=%async_computation.2 | async-start | bytes 2097152 | tf_op jit(solution)/shard_map/all_to_all | solution.py:107
  199.7 5.3 %copy-start.87 = (s32[64]{0:T(128)S(1)}, s32[64]{0:T(128)}, u32[]{:S(2)}) copy-start(s32[64]{0:T(128)} %copy-done.86) | copy-start | bytes 772
  199.7 5.3 %copy-start.100 = (s32[64,1]{0,1:T(1,128)S(1)}, s32[64,1]{0,1:T(1,128)}, u32[]{:S(2)}) copy-start(s32[64,1]{0,1:T(1,128)} %mul.452) | copy-start | bytes 772
  199.7 5.8 %copy-start.89 = (pred[32,2]{0,1:T(4,128)(4,1)S(1)}, pred[32,2]{0,1:T(4,128)(4,1)}, u32[]{:S(2)}) copy-start(pred[32,2]{0,1:T(4,128)(4,1)} %get-tuple-element.34) | copy-start | bytes 196
  199.7 6.4 %copy-start.82 = (f32[32,2]{0,1:T(2,128)S(1)}, f32[32,2]{0,1:T(2,128)}, u32[]{:S(2)}) copy-start(f32[32,2]{0,1:T(2,128)} %get-tuple-element.52) | copy-start | bytes 772
  199.7 7.1 %copy-start.77 = (s32[32,2]{0,1:T(2,128)S(1)}, s32[32,2]{0,1:T(2,128)}, u32[]{:S(2)}) copy-start(s32[32,2]{0,1:T(2,128)} %get-tuple-element.40) | copy-start | bytes 772
  199.7 7.1 %copy-start.83 = (f32[32,2]{0,1:T(2,128)S(1)}, f32[32,2]{0,1:T(2,128)}, u32[]{:S(2)}) copy-start(f32[32,2]{0,1:T(2,128)} %get-tuple-element.33) | copy-start | bytes 772
  199.7 21.5 %all-to-all-start.8 = ((bf16[32,8,2048]{2,1,0:T(8,128)(2,1)}), bf16[32,8,2048]{2,1,0:T(8,128)(2,1)}, u32[]{:S(2)}, u32[]{:S(2)}) async-start(bf16[32,8,2048]{2,1,0:T(8,128)(2,1)} %fusion.3), calls=%async_computation.8 | async-start | bytes 2097152 | tf_op jit(solution)/shard_map/all_to_all | solution.py:107
  209.8 22.1 %copy-start.10 = (f32[32,2048]{1,0:T(8,128)}, f32[32,2048]{1,0:T(8,128)S(1)}, u32[]{:S(2)}) copy-start(f32[32,2048]{1,0:T(8,128)S(1)} %fusion.47) | copy-start | bytes 786436
  226.5 50.0 %copy-start.93 = (f32[32]{0:T(128)}, f32[32]{0:T(128)S(1)}, u32[]{:S(2)}) copy-start(f32[32]{0:T(128)S(1)} %fusion.165) | copy-start | bytes 388
  226.5 7.7 %copy-start.66 = (f32[2]{0:T(128)S(1)}, f32[2]{0:T(128)}, u32[]{:S(2)}) copy-start(f32[2]{0:T(128)} %reduce_sum.334) | copy-start | bytes 28
  226.5 8.2 %copy-start.78 = (s32[32,2]{0,1:T(2,128)S(1)}, s32[32,2]{0,1:T(2,128)}, u32[]{:S(2)}) copy-start(s32[32,2]{0,1:T(2,128)} %get-tuple-element.75) | copy-start | bytes 772
  226.5 8.4 %copy-start.61 = (s32[32,2]{0,1:T(2,128)S(1)}, s32[32,2]{0,1:T(2,128)}, u32[]{:S(2)}) copy-start(s32[32,2]{0,1:T(2,128)} %copy-done.60) | copy-start | bytes 772
  226.6 8.4 %copy-start.99 = (pred[32,2]{0,1:T(4,128)(4,1)S(1)}, pred[32,2]{0,1:T(4,128)(4,1)}, u32[]{:S(2)}) copy-start(pred[32,2]{0,1:T(4,128)(4,1)} %iota_compare_fusion.11) | copy-start | bytes 196
  226.8 10.3 %copy-start.35 = (bf16[1,32,2048]{2,1,0:T(8,128)(2,1)S(1)}, bf16[1,32,2048]{2,1,0:T(8,128)(2,1)}, u32[]{:S(2)}) copy-start(bf16[1,32,2048]{2,1,0:T(8,128)(2,1)} %param.20) | copy-start | bytes 393220
  228.0 20.9 %all-to-all-start.4 = ((bf16[32,8,2048]{2,1,0:T(8,128)(2,1)}), bf16[32,8,2048]{2,1,0:T(8,128)(2,1)S(1)}, u32[]{:S(2)}, u32[]{:S(2)}) async-start(bf16[32,8,2048]{2,1,0:T(8,128)(2,1)} %bitcast.34), calls=%async_computation.4 | async-start | bytes 2097152 | tf_op jit(solution)/shard_map/all_to_all | solution.py:104
  232.6 4.5 %collective-permute-start = (bf16[32,2048]{1,0:T(8,128)(2,1)}, bf16[32,2048]{1,0:T(8,128)(2,1)S(1)}, u32[]{:S(2)}, u32[]{:S(2)}) collective-permute-start(bf16[32,2048]{1,0:T(8,128)(2,1)} %fusion.74), channel_id=1, source_target_pairs={{0,32},{32,64},{64,96},{96,128},{128,160},{160,192},{192,224},{224... | collective-permute-start | bytes 393224 | tf_op jit(solution)/shard_map/ppermute | solution.py:21
  235.1 19.4 %copy-start.96 = (f32[32]{0:T(128)S(1)}, f32[32]{0:T(128)}, u32[]{:S(2)}) copy-start(f32[32]{0:T(128)} %copy-done.95) | copy-start | bytes 388
  235.1 19.4 %copy-start.20 = (bf16[1,32,2048]{2,1,0:T(8,128)(2,1)S(1)}, bf16[1,32,2048]{2,1,0:T(8,128)(2,1)}, u32[]{:S(2)}) copy-start(bf16[1,32,2048]{2,1,0:T(8,128)(2,1)} %param.22) | copy-start | bytes 393220
  235.1 19.4 %copy-start.85 = (f32[32]{0:T(128)S(1)}, f32[32]{0:T(128)}, u32[]{:S(2)}) copy-start(f32[32]{0:T(128)} %copy-done.84) | copy-start | bytes 388
  238.2 18.3 %copy-start.81 = (s32[32,2,1]{0,1,2:T(2,128)S(1)}, s32[32,2,1]{0,1,2:T(2,128)}, u32[]{:S(2)}) copy-start(s32[32,2,1]{0,1,2:T(2,128)} %get-tuple-element.48) | copy-start | bytes 772
  238.2 18.5 %copy-start.75 = (f32[32,2]{0,1:T(2,128)S(1)}, f32[32,2]{0,1:T(2,128)}, u32[]{:S(2)}) copy-start(f32[32,2]{0,1:T(2,128)} %get-tuple-element.63) | copy-start | bytes 772
  238.3 20.6 %copy-start.80 = (s32[32,2,1]{0,1,2:T(2,128)S(1)}, s32[32,2,1]{0,1,2:T(2,128)}, u32[]{:S(2)}) copy-start(s32[32,2,1]{0,1,2:T(2,128)} %get-tuple-element.51) | copy-start | bytes 772
  238.3 20.8 %copy-start.88 = (pred[32,2]{0,1:T(4,128)(4,1)S(1)}, pred[32,2]{0,1:T(4,128)(4,1)}, u32[]{:S(2)}) copy-start(pred[32,2]{0,1:T(4,128)(4,1)} %get-tuple-element.27) | copy-start | bytes 196
  238.3 21.5 %copy-start.79 = (s32[32,2]{0,1:T(2,128)S(1)}, s32[32,2]{0,1:T(2,128)}, u32[]{:S(2)}) copy-start(s32[32,2]{0,1:T(2,128)} %get-tuple-element.55) | copy-start | bytes 772
  238.3 23.1 %copy-start.21 = (bf16[1,32,2048]{2,1,0:T(8,128)(2,1)S(1)}, bf16[1,32,2048]{2,1,0:T(8,128)(2,1)}, u32[]{:S(2)}) copy-start(bf16[1,32,2048]{2,1,0:T(8,128)(2,1)} %param.23) | copy-start | bytes 393220
  248.8 7.8 %copy-start.15 = (bf16[32,8,2048]{2,1,0:T(8,128)(2,1)}, bf16[32,8,2048]{2,1,0:T(8,128)(2,1)S(1)}, u32[]{:S(2)}) copy-start(bf16[32,8,2048]{2,1,0:T(8,128)(2,1)S(1)} %all-to-all-done.4) | copy-start | bytes 3145732
  250.0 21.4 %all-to-all-start.3 = ((bf16[32,8,2048]{2,1,0:T(8,128)(2,1)}), bf16[32,8,2048]{2,1,0:T(8,128)(2,1)}, u32[]{:S(2)}, u32[]{:S(2)}) async-start(bf16[32,8,2048]{2,1,0:T(8,128)(2,1)} %bitcast.28), calls=%async_computation.3 | async-start | bytes 2097152 | tf_op jit(solution)/shard_map/all_to_all | solution.py:104
  254.7 5.9 %copy-start.23 = (bf16[32,2048]{1,0:T(8,128)(2,1)}, bf16[32,2048]{1,0:T(8,128)(2,1)S(1)}, u32[]{:S(2)}) copy-start(bf16[32,2048]{1,0:T(8,128)(2,1)S(1)} %fusion.83) | copy-start | bytes 393220
  254.7 6.7 %collective-permute-start.1 = (bf16[32,2048]{1,0:T(8,128)(2,1)S(1)}, bf16[32,2048]{1,0:T(8,128)(2,1)S(1)}, u32[]{:S(2)}, u32[]{:S(2)}) collective-permute-start(bf16[32,2048]{1,0:T(8,128)(2,1)S(1)} %fusion.83), channel_id=1, source_target_pairs={{32,0},{64,32},{96,64},{128,96},{160,128},{192,160},{224,192},{256... | collective-permute-start | bytes 393224 | tf_op jit(solution)/shard_map/ppermute | solution.py:21
  261.4 11.2 %copy-start.25 = (bf16[32,2048]{1,0:T(8,128)(2,1)}, bf16[32,2048]{1,0:T(8,128)(2,1)S(1)}, u32[]{:S(2)}) copy-start(bf16[32,2048]{1,0:T(8,128)(2,1)S(1)} %collective-permute-done.1) | copy-start | bytes 393220
  272.6 20.9 %all-to-all-start.11 = ((bf16[32,8,2048]{2,1,0:T(8,128)(2,1)}), bf16[32,8,2048]{2,1,0:T(8,128)(2,1)S(1)}, u32[]{:S(2)}, u32[]{:S(2)}) async-start(bf16[32,8,2048]{2,1,0:T(8,128)(2,1)} %bitcast.67), calls=%async_computation.11 | async-start | bytes 2097152 | tf_op jit(solution)/shard_map/all_to_all | solution.py:104
  287.3 12.4 %copy-start.13 = (bf16[32,2048]{1,0:T(8,128)(2,1)S(1)}, bf16[32,2048]{1,0:T(8,128)(2,1)}, u32[]{:S(2)}) copy-start(bf16[32,2048]{1,0:T(8,128)(2,1)} %copy-done.12) | copy-start | bytes 393220
  287.3 12.4 %copy-start.32 = (f32[1,2048]{1,0:T(1,128)S(1)}, f32[1,2048]{1,0:T(1,128)}, u32[]{:S(2)}) copy-start(f32[1,2048]{1,0:T(1,128)} %param.26) | copy-start | bytes 24580
  287.3 12.4 %copy-start.38 = (bf16[1,2048,8]{1,2,0:T(8,128)(2,1)S(1)}, bf16[1,2048,8]{1,2,0:T(8,128)(2,1)}, u32[]{:S(2)}) copy-start(bf16[1,2048,8]{1,2,0:T(8,128)(2,1)} %param.27) | copy-start | bytes 98308
  287.3 12.4 %copy-start.98 = (f32[32]{0:T(128)S(1)}, f32[32]{0:T(128)}, u32[]{:S(2)}) copy-start(f32[32]{0:T(128)} %copy-done.97) | copy-start | bytes 388
  295.7 10.9 %all-to-all-start.13 = ((bf16[32,1,8]{2,1,0:T(2,128)(2,1)}), bf16[32,1,8]{2,1,0:T(2,128)(2,1)S(1)}, u32[]{:S(2)}, u32[]{:S(2)}) async-start(bf16[32,1,8]{2,1,0:T(2,128)(2,1)} %convert_element_type.413), calls=%async_computation.13 | async-start | bytes 32768 | tf_op jit(solution)/shard_map/all_to_all | solution.py:107
  299.9 6.8 %copy-start.29 = (s32[1024]{0:T(1024)S(1)}, s32[1024]{0:T(1024)}, u32[]{:S(2)}) copy-start(s32[1024]{0:T(1024)} %pad_clamp_fusion) | copy-start | bytes 12292
  310.4 11.4 %all-to-all-start.10 = ((bf16[32,1,8]{2,1,0:T(2,128)(2,1)}), bf16[32,1,8]{2,1,0:T(2,128)(2,1)S(1)}, u32[]{:S(2)}, u32[]{:S(2)}) async-start(bf16[32,1,8]{2,1,0:T(2,128)(2,1)} %copy.257), calls=%async_computation.10 | async-start | bytes 32768 | tf_op jit(solution)/shard_map/all_to_all | solution.py:104
  314.7 15.1 %copy-start.76 = (s32[32,2]{0,1:T(2,128)S(1)}, s32[32,2]{0,1:T(2,128)}, u32[]{:S(2)}) copy-start(s32[32,2]{0,1:T(2,128)} %get-tuple-element.39) | copy-start | bytes 772
  322.4 21.2 %all-to-all-start.5 = ((bf16[32,8,2048]{2,1,0:T(8,128)(2,1)}), bf16[32,8,2048]{2,1,0:T(8,128)(2,1)S(1)}, u32[]{:S(2)}, u32[]{:S(2)}) async-start(bf16[32,8,2048]{2,1,0:T(8,128)(2,1)} %slice_bitcast_fusion), calls=%async_computation.5 | async-start | bytes 2097152 | tf_op jit(solution)/shard_map/all_to_all | solution.py:107
  334.7 13.5 %copy-start.48 = (s32[1024]{0:T(1024)S(1)}, s32[1024]{0:T(1024)}, u32[]{:S(2)}) copy-start(s32[1024]{0:T(1024)} %pad_clamp_fusion.2) | copy-start | bytes 12292
  343.6 21.4 %all-to-all-start.12 = ((bf16[32,8,2048]{2,1,0:T(8,128)(2,1)}), bf16[32,8,2048]{2,1,0:T(8,128)(2,1)}, u32[]{:S(2)}, u32[]{:S(2)}) async-start(bf16[32,8,2048]{2,1,0:T(8,128)(2,1)} %fusion.2), calls=%async_computation.12 | async-start | bytes 2097152 | tf_op jit(solution)/shard_map/all_to_all | solution.py:107
  (55 other events, 109.4 us)
